TPU v7x, 32 devices: a whole 2x2x4 slice. The times are simulated.
32 devices in a mesh: seq: 8 (over z, core), dp: 4 (over y, x).
Axes of the slice: x: 2, y: 2, z: 4, core: 2. Of those that a mesh axis runs over, the one named last changes fastest.
Arguments:
- query_proj: bfloat16 [3072, 2560], P(('dp', 'seq')), parts along dimension 0, may hold values from -4.5 to 4.5
- key_proj: bfloat16 [3072, 2560], P(('dp', 'seq')), parts along dimension 0, may hold values from -4.5 to 4.5
- value_proj: bfloat16 [3072, 2560], P(('dp', 'seq')), parts along dimension 0, may hold values from -16 to 16
- token_rows: int32 [3072], P('dp'), parts along dimension 0, may hold values from 0 to 767, as said below
- key_tiles: int32 [64, 4], P(('dp', 'seq')), parts along dimension 0, may hold values from 0 to 15, as said below
- key_count: int32 [64], P(('dp', 'seq')), parts along dimension 0, may hold values from 1 to 4
Outputs:
- attended: bfloat16 [3072, 2560], P(('dp', 'seq')), parts along dimension 0
There are 4 independent parts, one for each index of `dp`. A program takes and returns all parts, laid end to end along the dimension named above; each array names one. Nothing has to cross between parts.
Inputs may be any that keep to these rules, and one draw needn't show every extreme that they name: token_rows is a permutation; the rows of every aligned block of 96 frame-slab rows go to every aligned block of 96 tile-order rows exactly 96 // 8 times. `key_tiles`: for query tile i the entries m < key_count[i] are distinct, include i, and each lies between 2 * (i // 2 - 2) and 2 * (i // 2 + 2) + 1; later entries equal i.
All inputs are finite; a program needn't handle non-finite values.
Results may differ from a plain program's by a relative error of at most 0.0049.
Values may be sent and summed in bfloat16 or wider, within the bound.
No kernel may reach another device: no remote copies, remote signals or barrier semaphores. Data moves between devices by JAX's collectives and lax.ppermute only.
A program may use at most 64 MiB of HBM per device.

v0:
```python
import jax
import jax.numpy as jnp
from jax import lax
from jax.sharding import PartitionSpec as P

HD = 128
KMAX = 4
REACH = 2


def passed_along(value, axis, by):
    size = lax.axis_size(axis)
    pairs = [(i, i + by) for i in range(size) if 0 <= i + by < size]
    return lax.ppermute(value, axis, pairs)


def order_for(inverse, owner_dev, rows_dev):
    sources = lax.dynamic_slice_in_dim(inverse, owner_dev * rows_dev, rows_dev) // rows_dev
    keyed = sources * rows_dev + jnp.arange(rows_dev, dtype=jnp.int32)
    return jnp.argsort(keyed)


def attend_heads(query_rows, key_rows, value_rows, allowed, head_count):
    last = query_rows.ndim - 1

    def one_head(head_index):
        start = head_index * HD
        query_head = lax.dynamic_slice_in_dim(query_rows, start, HD, last)
        key_head = lax.dynamic_slice_in_dim(key_rows, start, HD, last)
        value_head = lax.dynamic_slice_in_dim(value_rows, start, HD, last)
        scores = jnp.einsum(
            "...qd,...kd->...qk", query_head, key_head, preferred_element_type=jnp.float32
        ) * HD ** (-0.5)
        scores = jnp.where(allowed, scores, -jnp.inf)
        peak = jnp.max(scores, axis=-1, keepdims=True)
        exponent = jnp.exp(scores - peak)
        weights = (exponent / jnp.sum(exponent, axis=-1, keepdims=True)).astype(jnp.bfloat16)
        mixed = jnp.einsum(
            "...qk,...kd->...qd", weights, value_head, preferred_element_type=jnp.float32
        )
        return mixed.astype(jnp.bfloat16)

    return lax.map(one_head, jnp.arange(head_count))


def shards(query_proj, key_proj, value_proj, token_rows, key_tiles, key_count):
    members = lax.axis_size("seq")
    myself = lax.axis_index("seq")
    rows_dev = query_proj.shape[0]
    feat_width = query_proj.shape[1]
    per_peer = rows_dev // members
    tile_rows = rows_dev // 2
    head_count = feat_width // HD
    inverse = jnp.argsort(token_rows)
    own_dest = lax.dynamic_slice_in_dim(token_rows, myself * rows_dev, rows_dev)
    send_order = jnp.argsort(own_dest)
    sorted_query = query_proj[send_order].reshape(members, per_peer, feat_width)
    sorted_keys = key_proj[send_order].reshape(members, per_peer, feat_width)
    sorted_values = value_proj[send_order].reshape(members, per_peer, feat_width)
    order_own = order_for(inverse, myself, rows_dev)
    placement_own = jnp.argsort(order_own)
    arrived_query, arrived_keys, arrived_values = (
        lax.all_to_all(sorted_query, "seq", split_axis=0, concat_axis=0, tiled=True),
        lax.all_to_all(sorted_keys, "seq", split_axis=0, concat_axis=0, tiled=True),
        lax.all_to_all(sorted_values, "seq", split_axis=0, concat_axis=0, tiled=True),
    )
    query_tile = arrived_query.reshape(rows_dev, feat_width)[placement_own]
    key_tile = arrived_keys.reshape(rows_dev, feat_width)[placement_own]
    value_tile = arrived_values.reshape(rows_dev, feat_width)[placement_own]
    blocks = []
    for offset in range(-REACH, REACH + 1):
        if offset == 0:
            blocks.append((key_tile, value_tile))
        else:
            blocks.append(passed_along((key_tile, value_tile), "seq", -offset))
    window_keys = jnp.concatenate([pair[0] for pair in blocks], axis=0)
    window_values = jnp.concatenate([pair[1] for pair in blocks], axis=0)
    entry_live = jnp.arange(KMAX)[None, :] < key_count[:, None]
    window_ids = (
        (myself + jnp.arange(-REACH, REACH + 1))[:, None] * 2 + jnp.arange(2)[None, :]
    ).reshape(-1)
    matches = (key_tiles[:, :, None] == window_ids[None, None, :]) & entry_live[:, :, None]
    listed = jnp.any(matches, axis=1)
    allowed = jnp.repeat(jnp.repeat(listed, tile_rows, axis=0), tile_rows, axis=1)
    mixed = attend_heads(query_tile, window_keys, window_values, allowed, head_count)
    tile_out = jnp.moveaxis(mixed, 0, -2).reshape(rows_dev, feat_width)
    back_send = tile_out[order_own].reshape(members, per_peer, feat_width)
    arrived_back = lax.all_to_all(back_send, "seq", split_axis=0, concat_axis=0, tiled=True)
    return arrived_back.reshape(rows_dev, feat_width)[jnp.argsort(send_order)]


def solution(mesh):
    return jax.shard_map(
        shards,
        mesh=mesh,
        in_specs=(
            P(("dp", "seq"), None),
            P(("dp", "seq"), None),
            P(("dp", "seq"), None),
            P("dp"),
            P(("dp", "seq"), None),
            P(("dp", "seq")),
        ),
        out_specs=P(("dp", "seq"), None),
        check_vma=False,
    )
```

profile of v0, /device:TPU:0, one launch (start us, length us, event | category | flops | bytes accessed | tf_op | source)
XLA Modules:
  0.0 226.7 jit_solution(4143252565832732605)
XLA Ops:
  0.0 5.1 %sort.77 = (s32[768]{0:T(1024)}, s32[768]{0:T(1024)S(1)}) sort(s32[768]{0:T(1024)} %param.11, s32[768]{0:T(1024)S(1)} %iota.41), dimensions={0}, to_apply=%region_1.2 | sort | flops 7680 | bytes 12288 | tf_op jit(solution)/shard_map/jit(argsort)/sort | solution.py:54
  6.0 2.5 %sort.78 = (s32[96]{0:T(128)}, s32[96]{0:T(128)S(1)}) sort(s32[96]{0:T(128)S(1)} %iota_add_fusion.1, s32[96]{0:T(128)S(1)} %iota.43), dimensions={0}, to_apply=%region_2.3 | sort | flops 672 | bytes 1536 | tf_op jit(solution)/shard_map/jit(argsort)/sort | solution.py:20
  8.5 2.5 %sort.76 = (s32[96]{0:T(128)}, s32[96]{0:T(128)S(1)}) sort(s32[96]{0:T(128)S(1)} %dynamic_slice.19, s32[96]{0:T(128)S(1)} %iota.40), dimensions={0}, to_apply=%region_0.0 | sort | flops 672 | bytes 1536 | tf_op jit(solution)/shard_map/jit(argsort)/sort | solution.py:56
  12.9 6.4 %all-to-all-start.2 = ((bf16[8,12,2560]{2,1,0:T(8,128)(2,1)}), bf16[8,12,2560]{2,1,0:T(8,128)(2,1)S(1)}, u32[]{:S(2)}, u32[]{:S(2)}) async-start(bf16[8,12,2560]{2,1,0:T(8,128)(2,1)} %reshape.86), calls=%async_computation.2 | async-start | bytes 1310720 | tf_op jit(solution)/shard_map/all_to_all | solution.py:65
  21.1 16.3 %all-to-all-done.2 = bf16[8,12,2560]{2,1,0:T(8,128)(2,1)S(1)} async-done(((bf16[8,12,2560]{2,1,0:T(8,128)(2,1)}), bf16[8,12,2560]{2,1,0:T(8,128)(2,1)S(1)}, u32[]{:S(2)}, u32[]{:S(2)}) %all-to-all-start.2) | async-done | bytes 491552 | tf_op jit(solution)/shard_map/all_to_all | solution.py:65
  37.4 3.5 %all-to-all-start.1 = ((bf16[8,12,2560]{2,1,0:T(8,128)(2,1)}), bf16[8,12,2560]{2,1,0:T(8,128)(2,1)S(1)}, u32[]{:S(2)}, u32[]{:S(2)}) async-start(bf16[8,12,2560]{2,1,0:T(8,128)(2,1)} %reshape.82), calls=%async_computation.1 | async-start | bytes 1310720 | tf_op jit(solution)/shard_map/all_to_all | solution.py:64
  40.9 2.5 %sort.79 = (s32[96]{0:T(128)}, s32[96]{0:T(128)S(1)}) sort(s32[96]{0:T(128)S(1)} %get-tuple-element.49, s32[96]{0:T(128)S(1)} %iota.44), dimensions={0}, to_apply=%region_3.4 | sort | flops 672 | bytes 1536 | tf_op jit(solution)/shard_map/jit(argsort)/sort | solution.py:61
  45.3 13.7 %all-to-all-done.1 = bf16[8,12,2560]{2,1,0:T(8,128)(2,1)S(1)} async-done(((bf16[8,12,2560]{2,1,0:T(8,128)(2,1)}), bf16[8,12,2560]{2,1,0:T(8,128)(2,1)S(1)}, u32[]{:S(2)}, u32[]{:S(2)}) %all-to-all-start.1) | async-done | bytes 491552 | tf_op jit(solution)/shard_map/all_to_all | solution.py:64
  59.0 3.5 %all-to-all-start = ((bf16[8,12,2560]{2,1,0:T(8,128)(2,1)}), bf16[8,12,2560]{2,1,0:T(8,128)(2,1)S(1)}, u32[]{:S(2)}, u32[]{:S(2)}) async-start(bf16[8,12,2560]{2,1,0:T(8,128)(2,1)} %reshape.80), calls=%async_computation | async-start | bytes 1310720 | tf_op jit(solution)/shard_map/all_to_all | solution.py:63
  63.6 4.6 %collective-permute-start.4 = (bf16[96,2560]{1,0:T(8,128)(2,1)S(1)}, bf16[96,2560]{1,0:T(8,128)(2,1)}, u32[]{:S(2)}, u32[]{:S(2)}) collective-permute-start(bf16[96,2560]{1,0:T(8,128)(2,1)S(1)} %gather_fusion.5), channel_id=1, source_target_pairs={{0,8},{4,12},{8,16},{12,20},{16,24},{20,28},{1,9},{5,13},{9,17},{1... | collective-permute-start | bytes 1474568 | tf_op jit(solution)/shard_map/ppermute | solution.py:14
  68.3 2.5 %collective-permute-start.5 = (bf16[96,2560]{1,0:T(8,128)(2,1)S(1)}, bf16[96,2560]{1,0:T(8,128)(2,1)}, u32[]{:S(2)}, u32[]{:S(2)}) collective-permute-start(bf16[96,2560]{1,0:T(8,128)(2,1)S(1)} %gather_fusion.5), channel_id=1, source_target_pairs={{0,4},{4,8},{8,12},{12,16},{16,20},{20,24},{24,28},{1,5},{5,9},{9,... | collective-permute-start | bytes 1474568 | tf_op jit(solution)/shard_map/ppermute | solution.py:14
  71.3 1.3 collective-permute-start.6
  72.6 1.3 collective-permute-start.7
  74.9 5.8 %collective-permute-start = (bf16[96,2560]{1,0:T(8,128)(2,1)S(1)}, bf16[96,2560]{1,0:T(8,128)(2,1)}, u32[]{:S(2)}, u32[]{:S(2)}) collective-permute-start(bf16[96,2560]{1,0:T(8,128)(2,1)S(1)} %gather_fusion.3), channel_id=1, source_target_pairs={{0,8},{4,12},{8,16},{12,20},{16,24},{20,28},{1,9},{5,13},{9,17},{1... | collective-permute-start | bytes 1474568 | tf_op jit(solution)/shard_map/ppermute | solution.py:14
  82.2 2.7 %collective-permute-done.4 = bf16[96,2560]{1,0:T(8,128)(2,1)} collective-permute-done((bf16[96,2560]{1,0:T(8,128)(2,1)S(1)}, bf16[96,2560]{1,0:T(8,128)(2,1)}, u32[]{:S(2)}, u32[]{:S(2)}) %collective-permute-start.4) | collective-permute-done | bytes 491552 | tf_op jit(solution)/shard_map/ppermute | solution.py:14
  84.9 1.6 collective-permute-start.1
  86.5 1.8 constant_dynamic-update-slice_fusion.9
  88.4 1.3 collective-permute-start.2
  89.6 1.9 constant_dynamic-update-slice_fusion.8
  92.3 3.1 %collective-permute-done = bf16[96,2560]{1,0:T(8,128)(2,1)} collective-permute-done((bf16[96,2560]{1,0:T(8,128)(2,1)S(1)}, bf16[96,2560]{1,0:T(8,128)(2,1)}, u32[]{:S(2)}, u32[]{:S(2)}) %collective-permute-start) | collective-permute-done | bytes 491552 | tf_op jit(solution)/shard_map/ppermute | solution.py:14
  95.5 1.3 collective-permute-start.3
  97.9 1.9 constant_dynamic-update-slice_fusion.6
  99.8 1.9 constant_dynamic-update-slice_fusion.5
  101.7 13.1 %collective-permute-done.3 = bf16[96,2560]{1,0:T(8,128)(2,1)S(1)} collective-permute-done((bf16[96,2560]{1,0:T(8,128)(2,1)S(1)}, bf16[96,2560]{1,0:T(8,128)(2,1)S(1)}, u32[]{:S(2)}, u32[]{:S(2)}) %collective-permute-start.3) | collective-permute-done | bytes 491552 | tf_op jit(solution)/shard_map/ppermute | solution.py:14
  114.8 1.4 copy-done.3
  116.3 79.9 %while.11 = (s32[]{:T(128)}, bf16[20,96,128]{2,1,0:T(8,128)(2,1)S(1)}, s32[20]{0:T(128)S(1)}, bf16[96,2560]{1,0:T(8,128)(2,1)S(1)}, bf16[480,2560]{1,0:T(8,128)(...) while((s32[]{:T(128)}, ...), condition=%wide.region_8.9_spmd.clone, body=%wide.region_5.8_spmd.clone.sunk | while | flops 23973700 | bytes 1052395 | solution.py:43
  117.7 1.2 fusion.20
  133.7 1.2 fusion.20
  198.1 8.8 %all-to-all-start.3 = ((bf16[8,12,2560]{2,1,0:T(8,128)(2,1)}), bf16[8,12,2560]{2,1,0:T(8,128)(2,1)S(1)}, u32[]{:S(2)}, u32[]{:S(2)}) async-start(bf16[8,12,2560]{2,1,0:T(8,128)(2,1)} %reshape.89), calls=%async_computation.3 | async-start | bytes 1310720 | tf_op jit(solution)/shard_map/all_to_all | solution.py:88
  206.8 2.5 %sort.80 = (s32[96]{0:T(128)}, s32[96]{0:T(128)S(1)}) sort(s32[96]{0:T(128)S(1)} %get-tuple-element.47, s32[96]{0:T(128)S(1)} %iota.46), dimensions={0}, to_apply=%region_9.10 | sort | flops 672 | bytes 1536 | tf_op jit(solution)/shard_map/jit(argsort)/sort | solution.py:89
  209.4 15.6 %all-to-all-done.3 = bf16[8,12,2560]{2,1,0:T(8,128)(2,1)S(1)} async-done(((bf16[8,12,2560]{2,1,0:T(8,128)(2,1)}), bf16[8,12,2560]{2,1,0:T(8,128)(2,1)S(1)}, u32[]{:S(2)}, u32[]{:S(2)}) %all-to-all-start.3) | async-done | bytes 491552 | tf_op jit(solution)/shard_map/all_to_all | solution.py:88
  225.1 1.6 gather_fusion.7
  (183 shorter events, 78.0 us)
Async XLA Ops:
  0.0 11.1 %copy-start = (bf16[96,2560]{1,0:T(8,128)(2,1)S(1)}, bf16[96,2560]{1,0:T(8,128)(2,1)}, u32[]{:S(2)}) copy-start(bf16[96,2560]{1,0:T(8,128)(2,1)} %param.10) | copy-start | bytes 1474564
  11.1 8.2 %copy-start.1 = (bf16[96,2560]{1,0:T(8,128)(2,1)S(1)}, bf16[96,2560]{1,0:T(8,128)(2,1)}, u32[]{:S(2)}) copy-start(bf16[96,2560]{1,0:T(8,128)(2,1)} %param.9) | copy-start | bytes 1474564
  12.9 24.5 %all-to-all-start.2 = ((bf16[8,12,2560]{2,1,0:T(8,128)(2,1)}), bf16[8,12,2560]{2,1,0:T(8,128)(2,1)S(1)}, u32[]{:S(2)}, u32[]{:S(2)}) async-start(bf16[8,12,2560]{2,1,0:T(8,128)(2,1)} %reshape.86), calls=%async_computation.2 | async-start | bytes 1310720 | tf_op jit(solution)/shard_map/all_to_all | solution.py:65
  19.3 24.2 %copy-start.2 = (bf16[96,2560]{1,0:T(8,128)(2,1)S(1)}, bf16[96,2560]{1,0:T(8,128)(2,1)}, u32[]{:S(2)}) copy-start(bf16[96,2560]{1,0:T(8,128)(2,1)} %param.8) | copy-start | bytes 1474564
  37.4 21.6 %all-to-all-start.1 = ((bf16[8,12,2560]{2,1,0:T(8,128)(2,1)}), bf16[8,12,2560]{2,1,0:T(8,128)(2,1)S(1)}, u32[]{:S(2)}, u32[]{:S(2)}) async-start(bf16[8,12,2560]{2,1,0:T(8,128)(2,1)} %reshape.82), calls=%async_computation.1 | async-start | bytes 1310720 | tf_op jit(solution)/shard_map/all_to_all | solution.py:64
  59.0 22.2 %all-to-all-start = ((bf16[8,12,2560]{2,1,0:T(8,128)(2,1)}), bf16[8,12,2560]{2,1,0:T(8,128)(2,1)S(1)}, u32[]{:S(2)}, u32[]{:S(2)}) async-start(bf16[8,12,2560]{2,1,0:T(8,128)(2,1)} %reshape.80), calls=%async_computation | async-start | bytes 1310720 | tf_op jit(solution)/shard_map/all_to_all | solution.py:63
  62.7 8.1 %copy-start.6 = (s32[2]{0:T(128)S(1)}, s32[2]{0:T(128)}, u32[]{:S(2)}) copy-start(s32[2]{0:T(128)} %param.13) | copy-start | bytes 28
  62.7 8.2 %copy-start.5 = (s32[2,4]{1,0:T(2,128)S(1)}, s32[2,4]{1,0:T(2,128)}, u32[]{:S(2)}) copy-start(s32[2,4]{1,0:T(2,128)} %param.12) | copy-start | bytes 100
  63.6 21.3 %collective-permute-start.4 = (bf16[96,2560]{1,0:T(8,128)(2,1)S(1)}, bf16[96,2560]{1,0:T(8,128)(2,1)}, u32[]{:S(2)}, u32[]{:S(2)}) collective-permute-start(bf16[96,2560]{1,0:T(8,128)(2,1)S(1)} %gather_fusion.5), channel_id=1, source_target_pairs={{0,8},{4,12},{8,16},{12,20},{16,24},{20,28},{1,9},{5,13},{9,17},{1... | collective-permute-start | bytes 1474568 | tf_op jit(solution)/shard_map/ppermute | solution.py:14
  68.3 20.1 %collective-permute-start.5 = (bf16[96,2560]{1,0:T(8,128)(2,1)S(1)}, bf16[96,2560]{1,0:T(8,128)(2,1)}, u32[]{:S(2)}, u32[]{:S(2)}) collective-permute-start(bf16[96,2560]{1,0:T(8,128)(2,1)S(1)} %gather_fusion.5), channel_id=1, source_target_pairs={{0,4},{4,8},{8,12},{12,16},{16,20},{20,24},{24,28},{1,5},{5,9},{9,... | collective-permute-start | bytes 1474568 | tf_op jit(solution)/shard_map/ppermute | solution.py:14
  71.3 26.6 %collective-permute-start.6 = (bf16[96,2560]{1,0:T(8,128)(2,1)S(1)}, bf16[96,2560]{1,0:T(8,128)(2,1)}, u32[]{:S(2)}, u32[]{:S(2)}) collective-permute-start(bf16[96,2560]{1,0:T(8,128)(2,1)S(1)} %gather_fusion.5), channel_id=1, source_target_pairs={{4,0},{8,4},{12,8},{16,12},{20,16},{24,20},{28,24},{5,1},{9,5},{13... | collective-permute-start | bytes 1474568 | tf_op jit(solution)/shard_map/ppermute | solution.py:14
  72.6 27.2 %collective-permute-start.7 = (bf16[96,2560]{1,0:T(8,128)(2,1)S(1)}, bf16[96,2560]{1,0:T(8,128)(2,1)}, u32[]{:S(2)}, u32[]{:S(2)}) collective-permute-start(bf16[96,2560]{1,0:T(8,128)(2,1)S(1)} %gather_fusion.5), channel_id=1, source_target_pairs={{8,0},{12,4},{16,8},{20,12},{24,16},{28,20},{9,1},{13,5},{17,9},{2... | collective-permute-start | bytes 1474568 | tf_op jit(solution)/shard_map/ppermute | solution.py:14
  74.9 20.6 %collective-permute-start = (bf16[96,2560]{1,0:T(8,128)(2,1)S(1)}, bf16[96,2560]{1,0:T(8,128)(2,1)}, u32[]{:S(2)}, u32[]{:S(2)}) collective-permute-start(bf16[96,2560]{1,0:T(8,128)(2,1)S(1)} %gather_fusion.3), channel_id=1, source_target_pairs={{0,8},{4,12},{8,16},{12,20},{16,24},{20,28},{1,9},{5,13},{9,17},{1... | collective-permute-start | bytes 1474568 | tf_op jit(solution)/shard_map/ppermute | solution.py:14
  84.9 12.9 %collective-permute-start.1 = (bf16[96,2560]{1,0:T(8,128)(2,1)S(1)}, bf16[96,2560]{1,0:T(8,128)(2,1)S(1)}, u32[]{:S(2)}, u32[]{:S(2)}) collective-permute-start(bf16[96,2560]{1,0:T(8,128)(2,1)S(1)} %gather_fusion.3), channel_id=1, source_target_pairs={{0,4},{4,8},{8,12},{12,16},{16,20},{20,24},{24,28},{1,5},{5,9},{9,... | collective-permute-start | bytes 1474568 | tf_op jit(solution)/shard_map/ppermute | solution.py:14
  88.4 13.3 %collective-permute-start.2 = (bf16[96,2560]{1,0:T(8,128)(2,1)S(1)}, bf16[96,2560]{1,0:T(8,128)(2,1)S(1)}, u32[]{:S(2)}, u32[]{:S(2)}) collective-permute-start(bf16[96,2560]{1,0:T(8,128)(2,1)S(1)} %gather_fusion.3), channel_id=1, source_target_pairs={{4,0},{8,4},{12,8},{16,12},{20,16},{24,20},{28,24},{5,1},{9,5},{13... | collective-permute-start | bytes 1474568 | tf_op jit(solution)/shard_map/ppermute | solution.py:14
  95.5 19.3 %collective-permute-start.3 = (bf16[96,2560]{1,0:T(8,128)(2,1)S(1)}, bf16[96,2560]{1,0:T(8,128)(2,1)S(1)}, u32[]{:S(2)}, u32[]{:S(2)}) collective-permute-start(bf16[96,2560]{1,0:T(8,128)(2,1)S(1)} %gather_fusion.3), channel_id=1, source_target_pairs={{8,0},{12,4},{16,8},{20,12},{24,16},{28,20},{9,1},{13,5},{17,9},{2... | collective-permute-start | bytes 1474568 | tf_op jit(solution)/shard_map/ppermute | solution.py:14
  97.9 18.4 %copy-start.4 = (bf16[20,96,128]{2,1,0:T(8,128)(2,1)S(1)}, bf16[20,96,128]{2,1,0:T(8,128)(2,1)}, u32[]{:S(2)}) copy-start(bf16[20,96,128]{2,1,0:T(8,128)(2,1)} %custom-call.18) | copy-start | bytes 1474564
  114.8 1.4 copy-start.3
  198.1 26.9 %all-to-all-start.3 = ((bf16[8,12,2560]{2,1,0:T(8,128)(2,1)}), bf16[8,12,2560]{2,1,0:T(8,128)(2,1)S(1)}, u32[]{:S(2)}, u32[]{:S(2)}) async-start(bf16[8,12,2560]{2,1,0:T(8,128)(2,1)} %reshape.89), calls=%async_computation.3 | async-start | bytes 1310720 | tf_op jit(solution)/shard_map/all_to_all | solution.py:88
where the time goes:
time: 229 us; the launch traced here: 227 us
  waiting for transfers between devices  65 us (28%)
  matrix products  47.2 us (21%)
  starting transfers between devices  41.8 us (18%)
  local copies, waits for them, and re-layouts  38.8 us (17%)
  other arithmetic  19.6 us (9%)
  loops' own time  14 us (6%)
    dot_general x20, matrix products, one_head(): jnp.einsum('...qd,...kd->...qk', query_head, key_head, preferred_element_...  24.2 us
    dot_general x20, matrix products, one_head(): jnp.einsum('...qk,...kd->...qd', weights, value_head, preferred_element_t...  23 us
    ppermute x8, starting transfers between devices, passed_along(): return lax.ppermute(value, axis, pairs)  19.6 us
    ppermute x8, waiting for transfers between devices, passed_along(): return lax.ppermute(value, axis, pairs)  18.9 us
    all_to_all x1, waiting for transfers between devices, shards(): lax.all_to_all(sorted_values, 'seq', split_axis=0, concat_axis=0, tiled=T...  16.3 us
    all_to_all x1, waiting for transfers between devices, shards(): lax.all_to_all(back_send, 'seq', split_axis=0, concat_axis=0, tiled=True)  15.6 us
    another operation x1, loops' own time, attend_heads(): return lax.map(one_head, jnp.arange(head_count))  14 us
    all_to_all x1, waiting for transfers between devices, shards(): lax.all_to_all(sorted_keys, 'seq', split_axis=0, concat_axis=0, tiled=True)  13.7 us
  transfers between devices with their start and end apart: 12, of which 7 were waited for; matrix products, arithmetic and copies ran while one was open for 10% of the time, Pallas kernels for 0%

commit v1 on v0

--- a/solution.py
+++ b/solution.py
@@ -44,6 +44,26 @@
 
 
 def shards(query_proj, key_proj, value_proj, token_rows, key_tiles, key_count):
+
+    def order_chains(dim_k, axis_no, bus_axis, view):
+        p_next = lax.axis_size(bus_axis)
+        z2 = lax.axis_index(bus_axis)
+        long_array, local_part = (p_next, z2)
+        left_arr = view.shape[dim_k] // long_array
+        known = jnp.roll(view, -local_part * left_arr, axis=dim_k)
+        piece_next = lax.slice_in_dim(known, 0, left_arr, axis=dim_k)
+        src_i = 1
+        block_list = [piece_next]
+        while src_i < long_array:
+            val2 = lax.slice_in_dim(known, src_i * left_arr, (src_i + 1) * left_arr, axis=dim_k)
+            front = lax.ppermute(
+                val2, bus_axis, [(p, (p + src_i) % long_array) for p in range(long_array)]
+            )
+            block_list.append(front)
+            src_i += 1
+        near = jnp.concatenate(block_list[::-1], axis=axis_no)
+        return jnp.roll(near, (local_part + 1) * block_list[0].shape[axis_no], axis_no)
+
     members = lax.axis_size("seq")
     myself = lax.axis_index("seq")
     rows_dev = query_proj.shape[0]
@@ -62,7 +82,7 @@
     arrived_query, arrived_keys, arrived_values = (
         lax.all_to_all(sorted_query, "seq", split_axis=0, concat_axis=0, tiled=True),
         lax.all_to_all(sorted_keys, "seq", split_axis=0, concat_axis=0, tiled=True),
-        lax.all_to_all(sorted_values, "seq", split_axis=0, concat_axis=0, tiled=True),
+        order_chains(0, 0, "seq", sorted_values),
     )
     query_tile = arrived_query.reshape(rows_dev, feat_width)[placement_own]
     key_tile = arrived_keys.reshape(rows_dev, feat_width)[placement_own]

time: 229 us -> 218 us (0.952)
  waiting for transfers between devices: 65 us -> 50.7 us
  starting transfers between devices: 41.8 us -> 44.4 us
    all_to_all x1 -> x0, waiting for transfers between devices: 16.3 us -> none  [shards(): lax.all_to_all(sorted_values, 'seq', split_axis=0, concat_axis=0, tiled=T...]
    all_to_all x1, waiting for transfers between devices: 13.7 us -> 0.01 us  [shards(): lax.all_to_all(sorted_keys, 'seq', split_axis=0, concat_axis=0, tiled=True)]
    ppermute x0 -> x7, waiting for transfers between devices: none -> 13.5 us  [order_chains(): lax.ppermute(val2, bus_axis, [(p, (p + src_i) % long_array) for p in rang...]
    ppermute x0 -> x7, starting transfers between devices: none -> 10 us  [order_chains(): lax.ppermute(val2, bus_axis, [(p, (p + src_i) % long_array) for p in rang...]
    all_to_all x1 -> x0, starting transfers between devices: 6.35 us -> none  [shards(): lax.all_to_all(sorted_values, 'seq', split_axis=0, concat_axis=0, tiled=T...]
    all_to_all x1, starting transfers between devices: 8.77 us -> 3.54 us  [shards(): lax.all_to_all(back_send, 'seq', split_axis=0, concat_axis=0, tiled=True)]
    all_to_all x1, waiting for transfers between devices: 0.53 us -> 4.64 us  [shards(): lax.all_to_all(sorted_query, 'seq', split_axis=0, concat_axis=0, tiled=True)]
    all_to_all x1, starting transfers between devices: 3.54 us -> 7.44 us  [shards(): lax.all_to_all(sorted_query, 'seq', split_axis=0, concat_axis=0, tiled=True)]
  transfers between devices with their start and end apart: 12 -> 18, of which waited for: 7 -> 8; matrix products, arithmetic and copies ran while one was open for 10% -> 10% of each run, Pallas kernels for 0% -> 0%
where the time goes in v1:
time: 218 us; the launch traced here: 216 us
  waiting for transfers between devices  50.7 us (23%)
  matrix products  47.2 us (22%)
  starting transfers between devices  44.4 us (20%)
  local copies, waits for them, and re-layouts  39.1 us (18%)
  other arithmetic  20.2 us (9%)
  loops' own time  14 us (6%)
    dot_general x20, matrix products, one_head(): jnp.einsum('...qd,...kd->...qk', query_head, key_head, preferred_element_...  24.2 us
    dot_general x20, matrix products, one_head(): jnp.einsum('...qk,...kd->...qd', weights, value_head, preferred_element_t...  23 us
    ppermute x8, starting transfers between devices, passed_along(): return lax.ppermute(value, axis, pairs)  18.6 us
    ppermute x8, waiting for transfers between devices, passed_along(): return lax.ppermute(value, axis, pairs)  17 us
    all_to_all x1, waiting for transfers between devices, shards(): lax.all_to_all(back_send, 'seq', split_axis=0, concat_axis=0, tiled=True)  15.5 us
    another operation x1, loops' own time, attend_heads(): return lax.map(one_head, jnp.arange(head_count))  14 us
    ppermute x7, waiting for transfers between devices, order_chains(): lax.ppermute(val2, bus_axis, [(p, (p + src_i) % long_array) for p in rang...  13.5 us
    dynamic_slice x20, local copies, waits for them, and re-layouts, attend_heads(): return lax.map(one_head, jnp.arange(head_count))  11.7 us
  transfers between devices with their start and end apart: 18, of which 8 were waited for; matrix products, arithmetic and copies ran while one was open for 10% of the time, Pallas kernels for 0%

profile of v1, /device:TPU:0, one launch (start us, length us, event | category | flops | bytes accessed | tf_op | source)
XLA Modules:
  0.0 215.9 jit_solution(7567674167178901826)
XLA Ops:
  0.0 5.1 %sort.77 = (s32[768]{0:T(1024)}, s32[768]{0:T(1024)S(1)}) sort(s32[768]{0:T(1024)} %param.13, s32[768]{0:T(1024)S(1)} %iota.41), dimensions={0}, to_apply=%region_1.2 | sort | flops 7680 | bytes 12288 | tf_op jit(solution)/shard_map/jit(argsort)/sort | solution.py:74
  6.0 2.5 %sort.78 = (s32[96]{0:T(128)}, s32[96]{0:T(128)S(1)}) sort(s32[96]{0:T(128)S(1)} %iota_add_fusion.1, s32[96]{0:T(128)S(1)} %iota.43), dimensions={0}, to_apply=%region_2.3 | sort | flops 672 | bytes 1536 | tf_op jit(solution)/shard_map/jit(argsort)/sort | solution.py:20
  8.5 2.5 %sort.76 = (s32[96]{0:T(128)}, s32[96]{0:T(128)S(1)}) sort(s32[96]{0:T(128)S(1)} %dynamic_slice.22, s32[96]{0:T(128)S(1)} %iota.40), dimensions={0}, to_apply=%region_0.0 | sort | flops 672 | bytes 1536 | tf_op jit(solution)/shard_map/jit(argsort)/sort | solution.py:76
  12.4 4.6 %collective-permute-start.4 = (bf16[1,12,2560]{2,1,0:T(8,128)(2,1)S(1)}, bf16[1,12,2560]{2,1,0:T(8,128)(2,1)S(1)}, u32[]{:S(2)}, u32[]{:S(2)}) collective-permute-start(bf16[1,12,2560]{2,1,0:T(8,128)(2,1)S(1)} %get-tuple-element.93), channel_id=1, source_target_pairs={{0,28},{4,0},{8,4},{12,8},{16,12},{20,16},{24,20},{28,24},{1,29},{... | collective-permute-start | bytes 184328 | tf_op jit(solution)/shard_map/ppermute | solution.py:59
  17.6 2.7 %collective-permute-start.7 = (bf16[1,12,2560]{2,1,0:T(8,128)(2,1)S(1)}, bf16[1,12,2560]{2,1,0:T(8,128)(2,1)S(1)}, u32[]{:S(2)}, u32[]{:S(2)}) collective-permute-start(bf16[1,12,2560]{2,1,0:T(8,128)(2,1)S(1)} %get-tuple-element.90), channel_id=1, source_target_pairs={{0,16},{4,20},{8,24},{12,28},{16,0},{20,4},{24,8},{28,12},{1,17},{... | collective-permute-start | bytes 184328 | tf_op jit(solution)/shard_map/ppermute | solution.py:59
  22.1 4.7 %all-to-all-start.1 = ((bf16[8,12,2560]{2,1,0:T(8,128)(2,1)}), bf16[8,12,2560]{2,1,0:T(8,128)(2,1)S(1)}, u32[]{:S(2)}, u32[]{:S(2)}) async-start(bf16[8,12,2560]{2,1,0:T(8,128)(2,1)} %reshape.82), calls=%async_computation.1 | async-start | bytes 1310720 | tf_op jit(solution)/shard_map/all_to_all | solution.py:84
  26.8 2.5 %sort.79 = (s32[96]{0:T(128)}, s32[96]{0:T(128)S(1)}) sort(s32[96]{0:T(128)S(1)} %get-tuple-element.50, s32[96]{0:T(128)S(1)} %iota.44), dimensions={0}, to_apply=%region_3.4 | sort | flops 672 | bytes 1536 | tf_op jit(solution)/shard_map/jit(argsort)/sort | solution.py:81
  29.4 2.1 collective-permute-start.9
  31.7 13.2 %collective-permute-done.9 = bf16[1,12,2560]{2,1,0:T(8,128)(2,1)S(1)} collective-permute-done((bf16[1,12,2560]{2,1,0:T(8,128)(2,1)S(1)}, bf16[1,12,2560]{2,1,0:T(8,128)(2,1)S(1)}, u32[]{:S(2)}, u32[]{:S(2)}) %collective-permute-start.9) | collective-permute-done | bytes 61472 | tf_op jit(solution)/shard_map/ppermute | solution.py:59
  46.5 4.5 %collective-permute-start.11 = (bf16[96,2560]{1,0:T(8,128)(2,1)S(1)}, bf16[96,2560]{1,0:T(8,128)(2,1)S(1)}, u32[]{:S(2)}, u32[]{:S(2)}) collective-permute-start(bf16[96,2560]{1,0:T(8,128)(2,1)S(1)} %gather_fusion.5), channel_id=1, source_target_pairs={{0,8},{4,12},{8,16},{12,20},{16,24},{20,28},{1,9},{5,13},{9,17},{1... | collective-permute-start | bytes 1474568 | tf_op jit(solution)/shard_map/ppermute | solution.py:14
  51.2 2.5 %collective-permute-start.12 = (bf16[96,2560]{1,0:T(8,128)(2,1)S(1)}, bf16[96,2560]{1,0:T(8,128)(2,1)}, u32[]{:S(2)}, u32[]{:S(2)}) collective-permute-start(bf16[96,2560]{1,0:T(8,128)(2,1)S(1)} %gather_fusion.5), channel_id=1, source_target_pairs={{0,4},{4,8},{8,12},{12,16},{16,20},{20,24},{24,28},{1,5},{5,9},{9,... | collective-permute-start | bytes 1474568 | tf_op jit(solution)/shard_map/ppermute | solution.py:14
  56.0 1.3 collective-permute-start.13
  57.3 1.3 collective-permute-start.14
  58.6 4.0 %collective-permute-done.11 = bf16[96,2560]{1,0:T(8,128)(2,1)S(1)} collective-permute-done((bf16[96,2560]{1,0:T(8,128)(2,1)S(1)}, bf16[96,2560]{1,0:T(8,128)(2,1)S(1)}, u32[]{:S(2)}, u32[]{:S(2)}) %collective-permute-start.11) | collective-permute-done | bytes 491552 | tf_op jit(solution)/shard_map/ppermute | solution.py:14
  63.4 1.8 constant_dynamic-update-slice_fusion.15
  65.2 7.4 %all-to-all-start = ((bf16[8,12,2560]{2,1,0:T(8,128)(2,1)}), bf16[8,12,2560]{2,1,0:T(8,128)(2,1)S(1)}, u32[]{:S(2)}, u32[]{:S(2)}) async-start(bf16[8,12,2560]{2,1,0:T(8,128)(2,1)} %reshape.80), calls=%async_computation | async-start | bytes 1310720 | tf_op jit(solution)/shard_map/all_to_all | solution.py:83
  74.5 4.2 %collective-permute-start = (bf16[96,2560]{1,0:T(8,128)(2,1)S(1)}, bf16[96,2560]{1,0:T(8,128)(2,1)S(1)}, u32[]{:S(2)}, u32[]{:S(2)}) collective-permute-start(bf16[96,2560]{1,0:T(8,128)(2,1)S(1)} %gather_fusion.3), channel_id=1, source_target_pairs={{0,8},{4,12},{8,16},{12,20},{16,24},{20,28},{1,9},{5,13},{9,17},{1... | collective-permute-start | bytes 1474568 | tf_op jit(solution)/shard_map/ppermute | solution.py:14
  78.6 1.8 constant_dynamic-update-slice_fusion.13
  80.5 2.3 %collective-permute-start.1 = (bf16[96,2560]{1,0:T(8,128)(2,1)S(1)}, bf16[96,2560]{1,0:T(8,128)(2,1)}, u32[]{:S(2)}, u32[]{:S(2)}) collective-permute-start(bf16[96,2560]{1,0:T(8,128)(2,1)S(1)} %gather_fusion.3), channel_id=1, source_target_pairs={{0,4},{4,8},{8,12},{12,16},{16,20},{20,24},{24,28},{1,5},{5,9},{9,... | collective-permute-start | bytes 1474568 | tf_op jit(solution)/shard_map/ppermute | solution.py:14
  83.3 1.9 constant_dynamic-update-slice_fusion.12
  85.2 1.3 collective-permute-start.2
  86.4 1.3 collective-permute-start.3
  87.7 4.6 %all-to-all-done = bf16[8,12,2560]{2,1,0:T(8,128)(2,1)S(1)} async-done(((bf16[8,12,2560]{2,1,0:T(8,128)(2,1)}), bf16[8,12,2560]{2,1,0:T(8,128)(2,1)S(1)}, u32[]{:S(2)}, u32[]{:S(2)}) %all-to-all-start) | async-done | bytes 491552 | tf_op jit(solution)/shard_map/all_to_all | solution.py:83
  93.4 1.7 collective-permute-done
  97.3 10.9 %collective-permute-done.3 = bf16[96,2560]{1,0:T(8,128)(2,1)} collective-permute-done((bf16[96,2560]{1,0:T(8,128)(2,1)S(1)}, bf16[96,2560]{1,0:T(8,128)(2,1)}, u32[]{:S(2)}, u32[]{:S(2)}) %collective-permute-start.3) | collective-permute-done | bytes 491552 | tf_op jit(solution)/shard_map/ppermute | solution.py:14
  109.3 1.4 copy-done.3
  110.7 79.9 %while.11 = (s32[]{:T(128)}, bf16[20,96,128]{2,1,0:T(8,128)(2,1)S(1)}, s32[20]{0:T(128)S(1)}, bf16[96,2560]{1,0:T(8,128)(2,1)S(1)}, bf16[480,2560]{1,0:T(8,128)(...) while((s32[]{:T(128)}, ...), condition=%wide.region_8.10_spmd.clone, body=%wide.region_5.9_spmd.clone.sunk | while | flops 23973700 | bytes 1052395 | solution.py:43
  116.1 1.2 fusion.23
  192.5 3.5 %all-to-all-start.2 = ((bf16[8,12,2560]{2,1,0:T(8,128)(2,1)}), bf16[8,12,2560]{2,1,0:T(8,128)(2,1)S(1)}, u32[]{:S(2)}, u32[]{:S(2)}) async-start(bf16[8,12,2560]{2,1,0:T(8,128)(2,1)} %reshape.89), calls=%async_computation.2 | async-start | bytes 1310720 | tf_op jit(solution)/shard_map/all_to_all | solution.py:108
  196.1 2.5 %sort.80 = (s32[96]{0:T(128)}, s32[96]{0:T(128)S(1)}) sort(s32[96]{0:T(128)S(1)} %get-tuple-element.48, s32[96]{0:T(128)S(1)} %iota.46), dimensions={0}, to_apply=%region_9.11 | sort | flops 672 | bytes 1536 | tf_op jit(solution)/shard_map/jit(argsort)/sort | solution.py:109
  198.6 15.5 %all-to-all-done.2 = bf16[8,12,2560]{2,1,0:T(8,128)(2,1)S(1)} async-done(((bf16[8,12,2560]{2,1,0:T(8,128)(2,1)}), bf16[8,12,2560]{2,1,0:T(8,128)(2,1)S(1)}, u32[]{:S(2)}, u32[]{:S(2)}) %all-to-all-start.2) | async-done | bytes 491552 | tf_op jit(solution)/shard_map/all_to_all | solution.py:108
  214.2 1.6 gather_fusion.7
  (206 shorter events, 82.9 us)
Async XLA Ops:
  0.0 11.1 %copy-start = (bf16[96,2560]{1,0:T(8,128)(2,1)S(1)}, bf16[96,2560]{1,0:T(8,128)(2,1)}, u32[]{:S(2)}) copy-start(bf16[96,2560]{1,0:T(8,128)(2,1)} %param.12) | copy-start | bytes 1474564
  11.9 8.4 %copy-start.1 = (bf16[96,2560]{1,0:T(8,128)(2,1)S(1)}, bf16[96,2560]{1,0:T(8,128)(2,1)}, u32[]{:S(2)}) copy-start(bf16[96,2560]{1,0:T(8,128)(2,1)} %param.11) | copy-start | bytes 1474564
  12.4 17.0 %collective-permute-start.4 = (bf16[1,12,2560]{2,1,0:T(8,128)(2,1)S(1)}, bf16[1,12,2560]{2,1,0:T(8,128)(2,1)S(1)}, u32[]{:S(2)}, u32[]{:S(2)}) collective-permute-start(bf16[1,12,2560]{2,1,0:T(8,128)(2,1)S(1)} %get-tuple-element.93), channel_id=1, source_target_pairs={{0,28},{4,0},{8,4},{12,8},{16,12},{20,16},{24,20},{28,24},{1,29},{... | collective-permute-start | bytes 184328 | tf_op jit(solution)/shard_map/ppermute | solution.py:59
  17.0 14.5 %collective-permute-start.5 = (bf16[1,12,2560]{2,1,0:T(8,128)(2,1)S(1)}, bf16[1,12,2560]{2,1,0:T(8,128)(2,1)S(1)}, u32[]{:S(2)}, u32[]{:S(2)}) collective-permute-start(bf16[1,12,2560]{2,1,0:T(8,128)(2,1)S(1)} %get-tuple-element.92), channel_id=1, source_target_pairs={{0,24},{4,28},{8,0},{12,4},{16,8},{20,12},{24,16},{28,20},{1,25},{... | collective-permute-start | bytes 184328 | tf_op jit(solution)/shard_map/ppermute | solution.py:59
  17.6 14.0 %collective-permute-start.6 = (bf16[1,12,2560]{2,1,0:T(8,128)(2,1)S(1)}, bf16[1,12,2560]{2,1,0:T(8,128)(2,1)S(1)}, u32[]{:S(2)}, u32[]{:S(2)}) collective-permute-start(bf16[1,12,2560]{2,1,0:T(8,128)(2,1)S(1)} %get-tuple-element.91), channel_id=1, source_target_pairs={{0,20},{4,24},{8,28},{12,0},{16,4},{20,8},{24,12},{28,16},{1,21},{... | collective-permute-start | bytes 184328 | tf_op jit(solution)/shard_map/ppermute | solution.py:59
  17.6 14.0 %collective-permute-start.7 = (bf16[1,12,2560]{2,1,0:T(8,128)(2,1)S(1)}, bf16[1,12,2560]{2,1,0:T(8,128)(2,1)S(1)}, u32[]{:S(2)}, u32[]{:S(2)}) collective-permute-start(bf16[1,12,2560]{2,1,0:T(8,128)(2,1)S(1)} %get-tuple-element.90), channel_id=1, source_target_pairs={{0,16},{4,20},{8,24},{12,28},{16,0},{20,4},{24,8},{28,12},{1,17},{... | collective-permute-start | bytes 184328 | tf_op jit(solution)/shard_map/ppermute | solution.py:59
  20.3 11.3 %collective-permute-start.8 = (bf16[1,12,2560]{2,1,0:T(8,128)(2,1)S(1)}, bf16[1,12,2560]{2,1,0:T(8,128)(2,1)S(1)}, u32[]{:S(2)}, u32[]{:S(2)}) collective-permute-start(bf16[1,12,2560]{2,1,0:T(8,128)(2,1)S(1)} %get-tuple-element.89), channel_id=1, source_target_pairs={{0,12},{4,16},{8,20},{12,24},{16,28},{20,0},{24,4},{28,8},{1,13},{... | collective-permute-start | bytes 184328 | tf_op jit(solution)/shard_map/ppermute | solution.py:59
  22.1 43.1 %all-to-all-start.1 = ((bf16[8,12,2560]{2,1,0:T(8,128)(2,1)}), bf16[8,12,2560]{2,1,0:T(8,128)(2,1)S(1)}, u32[]{:S(2)}, u32[]{:S(2)}) async-start(bf16[8,12,2560]{2,1,0:T(8,128)(2,1)} %reshape.82), calls=%async_computation.1 | async-start | bytes 1310720 | tf_op jit(solution)/shard_map/all_to_all | solution.py:84
  29.4 15.4 %collective-permute-start.9 = (bf16[1,12,2560]{2,1,0:T(8,128)(2,1)S(1)}, bf16[1,12,2560]{2,1,0:T(8,128)(2,1)S(1)}, u32[]{:S(2)}, u32[]{:S(2)}) collective-permute-start(bf16[1,12,2560]{2,1,0:T(8,128)(2,1)S(1)} %get-tuple-element.88), channel_id=1, source_target_pairs={{0,8},{4,12},{8,16},{12,20},{16,24},{20,28},{24,0},{28,4},{1,9},{5... | collective-permute-start | bytes 184328 | tf_op jit(solution)/shard_map/ppermute | solution.py:59
  31.5 13.6 %collective-permute-start.10 = (bf16[1,12,2560]{2,1,0:T(8,128)(2,1)S(1)}, bf16[1,12,2560]{2,1,0:T(8,128)(2,1)S(1)}, u32[]{:S(2)}, u32[]{:S(2)}) collective-permute-start(bf16[1,12,2560]{2,1,0:T(8,128)(2,1)S(1)} %get-tuple-element.87), channel_id=1, source_target_pairs={{0,4},{4,8},{8,12},{12,16},{16,20},{20,24},{24,28},{28,0},{1,5},{5... | collective-permute-start | bytes 184328 | tf_op jit(solution)/shard_map/ppermute | solution.py:59
  45.6 5.6 %copy-start.6 = (s32[2]{0:T(128)S(1)}, s32[2]{0:T(128)}, u32[]{:S(2)}) copy-start(s32[2]{0:T(128)} %param.15) | copy-start | bytes 28
  45.6 8.1 %copy-start.5 = (s32[2,4]{1,0:T(2,128)S(1)}, s32[2,4]{1,0:T(2,128)}, u32[]{:S(2)}) copy-start(s32[2,4]{1,0:T(2,128)} %param.14) | copy-start | bytes 100
  45.6 8.2 %copy-start.2 = (bf16[96,2560]{1,0:T(8,128)(2,1)S(1)}, bf16[96,2560]{1,0:T(8,128)(2,1)}, u32[]{:S(2)}) copy-start(bf16[96,2560]{1,0:T(8,128)(2,1)} %param.10) | copy-start | bytes 1474564
  46.5 16.1 %collective-permute-start.11 = (bf16[96,2560]{1,0:T(8,128)(2,1)S(1)}, bf16[96,2560]{1,0:T(8,128)(2,1)S(1)}, u32[]{:S(2)}, u32[]{:S(2)}) collective-permute-start(bf16[96,2560]{1,0:T(8,128)(2,1)S(1)} %gather_fusion.5), channel_id=1, source_target_pairs={{0,8},{4,12},{8,16},{12,20},{16,24},{20,28},{1,9},{5,13},{9,17},{1... | collective-permute-start | bytes 1474568 | tf_op jit(solution)/shard_map/ppermute | solution.py:14
  51.2 12.2 %collective-permute-start.12 = (bf16[96,2560]{1,0:T(8,128)(2,1)S(1)}, bf16[96,2560]{1,0:T(8,128)(2,1)}, u32[]{:S(2)}, u32[]{:S(2)}) collective-permute-start(bf16[96,2560]{1,0:T(8,128)(2,1)S(1)} %gather_fusion.5), channel_id=1, source_target_pairs={{0,4},{4,8},{8,12},{12,16},{16,20},{20,24},{24,28},{1,5},{5,9},{9,... | collective-permute-start | bytes 1474568 | tf_op jit(solution)/shard_map/ppermute | solution.py:14
  56.0 22.7 %collective-permute-start.13 = (bf16[96,2560]{1,0:T(8,128)(2,1)S(1)}, bf16[96,2560]{1,0:T(8,128)(2,1)}, u32[]{:S(2)}, u32[]{:S(2)}) collective-permute-start(bf16[96,2560]{1,0:T(8,128)(2,1)S(1)} %gather_fusion.5), channel_id=1, source_target_pairs={{4,0},{8,4},{12,8},{16,12},{20,16},{24,20},{28,24},{5,1},{9,5},{13... | collective-permute-start | bytes 1474568 | tf_op jit(solution)/shard_map/ppermute | solution.py:14
  57.3 26.0 %collective-permute-start.14 = (bf16[96,2560]{1,0:T(8,128)(2,1)S(1)}, bf16[96,2560]{1,0:T(8,128)(2,1)}, u32[]{:S(2)}, u32[]{:S(2)}) collective-permute-start(bf16[96,2560]{1,0:T(8,128)(2,1)S(1)} %gather_fusion.5), channel_id=1, source_target_pairs={{8,0},{12,4},{16,8},{20,12},{24,16},{28,20},{9,1},{13,5},{17,9},{2... | collective-permute-start | bytes 1474568 | tf_op jit(solution)/shard_map/ppermute | solution.py:14
  65.2 27.2 %all-to-all-start = ((bf16[8,12,2560]{2,1,0:T(8,128)(2,1)}), bf16[8,12,2560]{2,1,0:T(8,128)(2,1)S(1)}, u32[]{:S(2)}, u32[]{:S(2)}) async-start(bf16[8,12,2560]{2,1,0:T(8,128)(2,1)} %reshape.80), calls=%async_computation | async-start | bytes 1310720 | tf_op jit(solution)/shard_map/all_to_all | solution.py:83
  74.5 20.6 %collective-permute-start = (bf16[96,2560]{1,0:T(8,128)(2,1)S(1)}, bf16[96,2560]{1,0:T(8,128)(2,1)S(1)}, u32[]{:S(2)}, u32[]{:S(2)}) collective-permute-start(bf16[96,2560]{1,0:T(8,128)(2,1)S(1)} %gather_fusion.3), channel_id=1, source_target_pairs={{0,8},{4,12},{8,16},{12,20},{16,24},{20,28},{1,9},{5,13},{9,17},{1... | collective-permute-start | bytes 1474568 | tf_op jit(solution)/shard_map/ppermute | solution.py:14
  80.5 14.6 %collective-permute-start.1 = (bf16[96,2560]{1,0:T(8,128)(2,1)S(1)}, bf16[96,2560]{1,0:T(8,128)(2,1)}, u32[]{:S(2)}, u32[]{:S(2)}) collective-permute-start(bf16[96,2560]{1,0:T(8,128)(2,1)S(1)} %gather_fusion.3), channel_id=1, source_target_pairs={{0,4},{4,8},{8,12},{12,16},{16,20},{20,24},{24,28},{1,5},{5,9},{9,... | collective-permute-start | bytes 1474568 | tf_op jit(solution)/shard_map/ppermute | solution.py:14
  85.2 11.0 %collective-permute-start.2 = (bf16[96,2560]{1,0:T(8,128)(2,1)S(1)}, bf16[96,2560]{1,0:T(8,128)(2,1)}, u32[]{:S(2)}, u32[]{:S(2)}) collective-permute-start(bf16[96,2560]{1,0:T(8,128)(2,1)S(1)} %gather_fusion.3), channel_id=1, source_target_pairs={{4,0},{8,4},{12,8},{16,12},{20,16},{24,20},{28,24},{5,1},{9,5},{13... | collective-permute-start | bytes 1474568 | tf_op jit(solution)/shard_map/ppermute | solution.py:14
  86.4 21.7 %collective-permute-start.3 = (bf16[96,2560]{1,0:T(8,128)(2,1)S(1)}, bf16[96,2560]{1,0:T(8,128)(2,1)}, u32[]{:S(2)}, u32[]{:S(2)}) collective-permute-start(bf16[96,2560]{1,0:T(8,128)(2,1)S(1)} %gather_fusion.3), channel_id=1, source_target_pairs={{8,0},{12,4},{16,8},{20,12},{24,16},{28,20},{9,1},{13,5},{17,9},{2... | collective-permute-start | bytes 1474568 | tf_op jit(solution)/shard_map/ppermute | solution.py:14
  93.4 17.3 %copy-start.4 = (bf16[20,96,128]{2,1,0:T(8,128)(2,1)S(1)}, bf16[20,96,128]{2,1,0:T(8,128)(2,1)}, u32[]{:S(2)}) copy-start(bf16[20,96,128]{2,1,0:T(8,128)(2,1)} %custom-call.19) | copy-start | bytes 1474564
  109.3 1.4 copy-start.3
  192.5 21.6 %all-to-all-start.2 = ((bf16[8,12,2560]{2,1,0:T(8,128)(2,1)}), bf16[8,12,2560]{2,1,0:T(8,128)(2,1)S(1)}, u32[]{:S(2)}, u32[]{:S(2)}) async-start(bf16[8,12,2560]{2,1,0:T(8,128)(2,1)} %reshape.89), calls=%async_computation.2 | async-start | bytes 1310720 | tf_op jit(solution)/shard_map/all_to_all | solution.py:108
